TPU v7x, 32 devices: a whole 2x2x4 slice. The times are simulated.
32 devices in a mesh: groups: 1, wide: 8 (over y, x, core), narrow: 4 (over z).
Axes of the slice: x: 2, y: 2, z: 4, core: 2. Of those that a mesh axis runs over, the one named last changes fastest.
Arguments:
- table_cells: bfloat16 [128, 128, 192], P(('groups', 'wide', 'narrow')), may hold values from -12 to 12
- counts: int32 [128], P(('groups', 'wide', 'narrow')), may hold values from 32 to 128, as said below
- train_count: int32 [1], P('groups'), may hold values from 32 to 96
- norm_gain: float32 [3, 192], replicated, may hold values from 0.5 to 1.5
- feature_in: bfloat16 [192, 576], P('narrow'), may hold values from -0.4375 to 0.4375
- feature_out: bfloat16 [192, 192], P('narrow'), may hold values from -0.4375 to 0.4375
- sample_in: bfloat16 [192, 576], P('narrow'), may hold values from -0.4375 to 0.4375
- sample_out: bfloat16 [192, 192], P('narrow'), may hold values from -0.4375 to 0.4375
- hidden_up: bfloat16 [192, 768], P('narrow'), may hold values from -0.4375 to 0.4375
- hidden_down: bfloat16 [768, 192], P('narrow'), may hold values from -0.21875 to 0.21875
Outputs:
- updated_cells: bfloat16 [128, 128, 192], P(('groups', 'wide', 'narrow'))
Inputs may be any that keep to these rules, and one draw needn't show every extreme that they name: `counts`: feature j of a row is present when j < its count; some row has all 128 features present. Rows 0 to train_count - 1 are the training rows.
All inputs are finite; a program needn't handle non-finite values.
Results may differ from a plain program's by a relative error of at most 0.0086.
Values may be sent and summed in bfloat16 or wider, within the bound.
A program may use at most 64 MiB of HBM per device.

v0:
```python
import jax
import jax.numpy as jnp
from jax import lax
from jax.sharding import PartitionSpec as P

HEADS = 6
epsilon = 1e-05


def normalize(values, gain):
    average = jnp.mean(values, axis=-1, keepdims=True)
    centered = values - average
    spread = jnp.mean(centered * centered, axis=-1, keepdims=True)
    return centered * lax.rsqrt(spread + epsilon) * gain


def attend(packed, valid, head_count):
    length = packed.shape[0]
    model_width = packed.shape[1] // 3
    head_size = model_width // head_count
    scale_factor = 1.0 / jnp.sqrt(jnp.float32(head_size))
    queries = packed[:, :model_width].reshape(length, head_count, head_size)
    key_part = packed[:, model_width : 2 * model_width].reshape(length, head_count, head_size)
    value_part = packed[:, 2 * model_width :].reshape(length, head_count, head_size)
    scores = (
        jnp.einsum("qhd,khd->hqk", queries, key_part, preferred_element_type=jnp.float32)
        * scale_factor
    )
    scores = jnp.where(valid[None, None, :], scores, jnp.float32(-1e30))
    maxima = jnp.max(scores, axis=-1, keepdims=True)
    exponentials = jnp.where(valid[None, None, :], jnp.exp(scores - maxima), jnp.float32(0.0))
    totals = jnp.sum(exponentials, axis=-1, keepdims=True)
    probabilities = (exponentials / totals).astype(jnp.bfloat16)
    context = jnp.einsum(
        "hqk,khd->qhd", probabilities, value_part, preferred_element_type=jnp.float32
    )
    return context.reshape(length, model_width).astype(jnp.bfloat16)


def project(values, weight):
    flat = values.reshape(-1, values.shape[-1])
    return jnp.dot(flat, weight, preferred_element_type=jnp.float32).reshape(
        values.shape[:-1] + (weight.shape[1],)
    )


def body(
    table_cells,
    counts,
    train_count,
    norm_gain,
    feature_in,
    feature_out,
    sample_in,
    sample_out,
    hidden_up,
    hidden_down,
):
    row_local, feats_all, model_width = table_cells.shape
    feat_in_all, feat_out_all = (
        lax.all_gather(feature_in, "narrow", axis=0, tiled=True),
        lax.all_gather(feature_out, "narrow", axis=0, tiled=True),
    )
    feature_ids = jnp.arange(feats_all, dtype=jnp.int32)
    packed = project(table_cells, feat_in_all).astype(jnp.bfloat16)

    def feature_row(pair):
        return attend(pair[0], feature_ids < pair[1], HEADS)

    context = lax.map(feature_row, (packed, counts))
    update = project(context, feat_out_all)
    first = normalize(table_cells.astype(jnp.float32) + update, norm_gain[0]).astype(jnp.bfloat16)
    columns = lax.all_to_all(first, ("wide", "narrow"), split_axis=1, concat_axis=0, tiled=True)
    rows_all, feat_local = (columns.shape[0], columns.shape[1])
    samp_in_all, samp_out_all = (
        lax.all_gather(sample_in, "narrow", axis=0, tiled=True),
        lax.all_gather(sample_out, "narrow", axis=0, tiled=True),
    )
    by_feature = jnp.swapaxes(columns, 0, 1)
    valid = jnp.arange(rows_all, dtype=jnp.int32) < train_count[0]
    packed_samples = project(by_feature, samp_in_all).astype(jnp.bfloat16)
    sample_context = lax.map(lambda column: attend(column, valid, HEADS), packed_samples)
    sample_update = project(sample_context, samp_out_all)
    second = normalize(by_feature.astype(jnp.float32) + sample_update, norm_gain[1]).astype(
        jnp.bfloat16
    )
    up_all, down_all = (
        lax.all_gather(hidden_up, "narrow", axis=0, tiled=True),
        lax.all_gather(hidden_down, "narrow", axis=0, tiled=True),
    )
    hidden = jax.nn.gelu(project(second, up_all), approximate=False).astype(jnp.bfloat16)
    back = project(hidden, down_all)
    result = normalize(second.astype(jnp.float32) + back, norm_gain[2]).astype(jnp.bfloat16)
    result_rows = jnp.swapaxes(result, 0, 1)
    return lax.all_to_all(result_rows, ("wide", "narrow"), split_axis=0, concat_axis=1, tiled=True)


def solution(mesh):
    return jax.shard_map(
        body,
        mesh=mesh,
        in_specs=(
            P(("groups", "wide", "narrow"), None, None),
            P(("groups", "wide", "narrow")),
            P("groups"),
            P(),
            P("narrow", None),
            P("narrow", None),
            P("narrow", None),
            P("narrow", None),
            P("narrow", None),
            P("narrow", None),
        ),
        out_specs=P(("groups", "wide", "narrow"), None, None),
        check_vma=False,
    )
```

profile of v0, /device:TPU:0, one launch (start us, length us, event | category | flops | bytes accessed | tf_op | source)
XLA Modules:
  0.0 134.4 jit_solution(16577640377260590868)
XLA Ops:
  0.0 0.8 fusion.94
  0.8 15.2 %all_gather.19 = bf16[192,192]{1,0:T(8,128)(2,1)S(1)} all-gather(bf16[48,192]{1,0:T(8,128)(2,1)} %param.19), channel_id=1, replica_groups=mesh['groups'=1,'wide'=8,'narrow'=4] {'narrow'}, dimensions={0}, use_global_device_ids=true | all-gather | bytes 92160 | tf_op jit(solution)/shard_map/all_gather | solution.py:62
  16.0 14.4 %all_gather.18 = bf16[192,576]{1,0:T(8,128)(2,1)S(1)} all-gather(bf16[48,576]{1,0:T(8,128)(2,1)} %param.18), channel_id=1, replica_groups=mesh['groups'=1,'wide'=8,'narrow'=4] {'narrow'}, dimensions={0}, use_global_device_ids=true | all-gather | bytes 276480 | tf_op jit(solution)/shard_map/all_gather | solution.py:61
  30.5 1.3 convolution_convert_fusion.3
  31.8 9.3 %while.22 = (s32[]{:T(128)}, bf16[4,128,192]{1,2,0:T(8,128)(2,1)S(1)}, bf16[4,128,576]{1,2,0:T(8,128)(2,1)S(1)}, s32[4]{0:T(128)S(1)}, s32[]{:T(128)}) while((s32[]{:T(128)}, bf16[4,128,192]{1,2,0:T(8,128)(2,1)S(1)}, bf16[4,128,576]{1,2,0:T(8,128)(2,1)S(1)}, s32[4]{0:T(128)S(1)}, s32[]{:T(128)}) %tuple.61), condition=%wide.region_3.4_spmd.clone, body=%wide.region_0.3_spmd.clone.sunk | while | flops 19981440 | bytes 1776221 | solution.py:70
  31.8 0.7 dynamic_slice.20
  32.5 0.7 iota_compare_fusion.4
  33.2 0.4 fusion.137
  33.6 0.3 fusion.138
  34.1 0.7 dynamic_slice.20
  34.8 0.7 iota_compare_fusion.4
  35.6 0.4 fusion.137
  35.9 0.3 fusion.138
  36.5 0.7 dynamic_slice.20
  37.1 0.7 iota_compare_fusion.4
  37.9 0.4 fusion.137
  38.2 0.3 fusion.138
  38.8 0.7 dynamic_slice.20
  39.5 0.7 iota_compare_fusion.4
  40.2 0.4 fusion.137
  40.6 0.3 fusion.138
  41.1 0.3 fusion.95
  41.6 0.9 copy.28
  42.5 5.3 %all-to-all-start = ((bf16[4,128,192]{2,0,1:T(4,128)(2,1)}), bf16[4,128,192]{2,0,1:T(4,128)(2,1)S(1)}, u32[]{:S(2)}, u32[]{:S(2)}) async-start(bf16[4,128,192]{2,0,1:T(4,128)(2,1)} %copy.28), calls=%async_computation | async-start | bytes 524288 | tf_op jit(solution)/shard_map/all_to_all | solution.py:73
  47.8 16.4 %all_gather.21 = bf16[192,192]{1,0:T(8,128)(2,1)S(1)} all-gather(bf16[48,192]{1,0:T(8,128)(2,1)S(1)} %copy-done.4), channel_id=1, replica_groups=mesh['groups'=1,'wide'=8,'narrow'=4] {'narrow'}, dimensions={0}, use_global_device_ids=true | all-gather | bytes 92160 | tf_op jit(solution)/shard_map/all_gather | solution.py:77
  64.3 13.8 %all_gather.20 = bf16[192,576]{1,0:T(8,128)(2,1)S(1)} all-gather(bf16[48,576]{1,0:T(8,128)(2,1)S(1)} %copy-done.3), channel_id=1, replica_groups=mesh['groups'=1,'wide'=8,'narrow'=4] {'narrow'}, dimensions={0}, use_global_device_ids=true | all-gather | bytes 276480 | tf_op jit(solution)/shard_map/all_gather | solution.py:76
  78.1 14.3 %all_gather.22 = bf16[192,768]{1,0:T(8,128)(2,1)S(1)} all-gather(bf16[48,768]{1,0:T(8,128)(2,1)S(1)} %copy-done.2), channel_id=1, replica_groups=mesh['groups'=1,'wide'=8,'narrow'=4] {'narrow'}, dimensions={0}, use_global_device_ids=true | all-gather | bytes 368640 | tf_op jit(solution)/shard_map/all_gather | solution.py:88
  92.3 14.2 %all_gather.23 = bf16[768,192]{1,0:T(8,128)(2,1)S(1)} all-gather(bf16[192,192]{1,0:T(8,128)(2,1)S(1)} %copy-done.1), channel_id=1, replica_groups=mesh['groups'=1,'wide'=8,'narrow'=4] {'narrow'}, dimensions={0}, use_global_device_ids=true | all-gather | bytes 368640 | tf_op jit(solution)/shard_map/all_gather | solution.py:89
  106.9 0.4 convolution_convert_fusion.2
  107.3 6.4 %while.23 = (s32[]{:T(128)}, bf16[4,128,192]{1,2,0:T(8,128)(2,1)S(1)}, bf16[4,128,576]{1,2,0:T(8,128)(2,1)S(1)}, s32[]{:T(128)}, s32[]{:T(128)}) while((s32[]{:T(128)}, bf16[4,128,192]{1,2,0:T(8,128)(2,1)S(1)}, bf16[4,128,576]{1,2,0:T(8,128)(2,1)S(1)}, s32[]{:T(128)}, s32[]{:T(128)}) %tuple.58), condition=%wide.region_9.10_spmd.clone, body=%wide.region_6.9_spmd.clone.sunk | while | flops 19981440 | bytes 1776209 | solution.py:82
  107.3 0.7 iota_compare_fusion.5
  108.0 0.4 fusion.146
  108.4 0.3 fusion.147
  108.6 0.2 convolution_convert_fusion.7
  108.9 0.7 iota_compare_fusion.5
  109.6 0.4 fusion.146
  110.0 0.3 fusion.147
  110.5 0.7 iota_compare_fusion.5
  111.2 0.4 fusion.146
  111.6 0.3 fusion.147
  112.1 0.7 iota_compare_fusion.5
  112.8 0.4 fusion.146
  113.2 0.3 fusion.147
  113.7 0.3 fusion.52
  114.2 0.8 fusion.43
  115.0 3.8 %fusion.46 = (f32[4,128]{1,0:T(4,128)S(1)}, f32[4,128,192]{1,2,0:T(8,128)S(1)}) fusion(bf16[4,128,192]{1,2,0:T(8,128)(2,1)S(1)} %multiply_convert_fusion, bf16[768,192]{1,0:T(8,128)(2,1)S(1)} %all_gather.23, f32[4,128,768]{2,1,0:T(8,128)S(1)} %get-tuple-element.114, u8[128,768]{1,0:T(8,128)(4,1)S(1)} %get-tuple-element.78, ...), kind=kOutput, calls=%fused_computation.80 | convolution fusion | flops 178814464 | bytes 2656256 | tf_op jit(solution)/shard_map/dot_general | solution.py:42
  119.2 14.2 %all_to_all.36 = bf16[128,4,192]{2,1,0:T(4,128)(2,1)S(1)} all-to-all(bf16[128,4,192]{2,1,0:T(4,128)(2,1)S(1)} %copy.33), channel_id=1, replica_groups=mesh['groups'=1,'wide'=8,'narrow'=4] {'wide','narrow'}, dimensions={0} | all-to-all | bytes 393216 | tf_op jit(solution)/shard_map/all_to_all | solution.py:95
  133.6 0.9 copy.35
  (62 shorter events, 3.4 us)
Async XLA Ops:
  0.0 31.8 %copy-start.5 = (s32[4]{0:T(128)S(1)}, s32[4]{0:T(128)}, u32[]{:S(2)}) copy-start(s32[4]{0:T(128)} %param.15) | copy-start | bytes 52
  31.8 9.3 %copy-start = (bf16[4,128,192]{1,2,0:T(8,128)(2,1)S(1)}, bf16[4,128,192]{1,2,0:T(8,128)(2,1)}, u32[]{:S(2)}) copy-start(bf16[4,128,192]{1,2,0:T(8,128)(2,1)} %param.14) | copy-start | bytes 589828
  41.1 6.7 %copy-start.4 = (bf16[48,192]{1,0:T(8,128)(2,1)S(1)}, bf16[48,192]{1,0:T(8,128)(2,1)}, u32[]{:S(2)}) copy-start(bf16[48,192]{1,0:T(8,128)(2,1)} %param.21) | copy-start | bytes 55300
  41.1 23.2 %copy-start.3 = (bf16[48,576]{1,0:T(8,128)(2,1)S(1)}, bf16[48,576]{1,0:T(8,128)(2,1)}, u32[]{:S(2)}) copy-start(bf16[48,576]{1,0:T(8,128)(2,1)} %param.20) | copy-start | bytes 165892
  41.1 36.9 %copy-start.2 = (bf16[48,768]{1,0:T(8,128)(2,1)S(1)}, bf16[48,768]{1,0:T(8,128)(2,1)}, u32[]{:S(2)}) copy-start(bf16[48,768]{1,0:T(8,128)(2,1)} %param.22) | copy-start | bytes 221188
  41.4 50.9 %copy-start.1 = (bf16[192,192]{1,0:T(8,128)(2,1)S(1)}, bf16[192,192]{1,0:T(8,128)(2,1)}, u32[]{:S(2)}) copy-start(bf16[192,192]{1,0:T(8,128)(2,1)} %param.23) | copy-start | bytes 221188
  42.5 64.1 %all-to-all-start = ((bf16[4,128,192]{2,0,1:T(4,128)(2,1)}), bf16[4,128,192]{2,0,1:T(4,128)(2,1)S(1)}, u32[]{:S(2)}, u32[]{:S(2)}) async-start(bf16[4,128,192]{2,0,1:T(4,128)(2,1)} %copy.28), calls=%async_computation | async-start | bytes 524288 | tf_op jit(solution)/shard_map/all_to_all | solution.py:73
where the time goes:
time: 135 us; the launch traced here: 134 us
  blocking collectives  103 us (76%)
  matrix products  13.6 us (10%)
  local copies, waits for them, and re-layouts  6.32 us (5%)
  other arithmetic  5.99 us (4%)
  starting transfers between devices  5.33 us (4%)
    all_gather x1, blocking collectives, body(): lax.all_gather(sample_out, 'narrow', axis=0, tiled=True)  16.4 us
    all_gather x1, blocking collectives, body(): lax.all_gather(feature_out, 'narrow', axis=0, tiled=True)  15.2 us
    all_gather x1, blocking collectives, body(): lax.all_gather(feature_in, 'narrow', axis=0, tiled=True)  14.4 us
    all_gather x1, blocking collectives, body(): lax.all_gather(hidden_up, 'narrow', axis=0, tiled=True)  14.3 us
    all_to_all x1, blocking collectives, body(): lax.all_to_all(result_rows, ('wide', 'narrow'), split_axis=0, concat_axis...  14.2 us
    all_gather x1, blocking collectives, body(): lax.all_gather(hidden_down, 'narrow', axis=0, tiled=True)  14.2 us
    all_gather x1, blocking collectives, body(): lax.all_gather(sample_in, 'narrow', axis=0, tiled=True)  13.8 us
    dot_general x6, matrix products, project(): jnp.dot(flat, weight, preferred_element_type=jnp.float32)  6.72 us
  transfers between devices with their start and end apart: 1, of which 0 were waited for; matrix products, arithmetic and copies ran while one was open for 0% of the time, Pallas kernels for 0%

commit v1 on v0

--- a/solution.py
+++ b/solution.py
@@ -5,6 +5,13 @@
 
 HEADS = 6
 epsilon = 1e-05
+
+
+def exchange_blocks(shard, name, split, join):
+    size = lax.axis_size(name)
+    blocks = jnp.stack(jnp.split(shard, size, axis=split), axis=0)
+    blocks = lax.all_to_all(blocks, name, split_axis=0, concat_axis=0)
+    return jnp.concatenate(blocks, axis=join)
 
 
 def normalize(values, gain):
@@ -92,7 +99,7 @@
     back = project(hidden, down_all)
     result = normalize(second.astype(jnp.float32) + back, norm_gain[2]).astype(jnp.bfloat16)
     result_rows = jnp.swapaxes(result, 0, 1)
-    return lax.all_to_all(result_rows, ("wide", "narrow"), split_axis=0, concat_axis=1, tiled=True)
+    return exchange_blocks(result_rows, ("wide", "narrow"), 0, 1)
 
 
 def solution(mesh):

time: 135 us -> 166 us (1.23)
  local copies, waits for them, and re-layouts: 6.32 us -> 37.5 us
    unnamed x12 -> x43, local copies, waits for them, and re-layouts: 0.04 us -> 24.7 us
    another operation x2 -> x4, local copies, waits for them, and re-layouts: 0.06 us -> 6.75 us  [the longest x2 6.69 us: exchange_blocks(): blocks = jnp.stack(jnp.split(shard, size, axis=split), axis=0)]
where the time goes in v1:
time: 166 us
  blocking collectives  103 us (62%)
  local copies, waits for them, and re-layouts  37.5 us (23%)
  matrix products  13.6 us (8%)
  other arithmetic  6 us (4%)
  starting transfers between devices  5.33 us (3%)
    unnamed x43, local copies, waits for them, and re-layouts  24.7 us
    all_gather x1, blocking collectives, body(): lax.all_gather(sample_out, 'narrow', axis=0, tiled=True)  16.4 us
    all_gather x1, blocking collectives, body(): lax.all_gather(feature_out, 'narrow', axis=0, tiled=True)  15.2 us
    all_gather x1, blocking collectives, body(): lax.all_gather(feature_in, 'narrow', axis=0, tiled=True)  14.4 us
    all_gather x1, blocking collectives, body(): lax.all_gather(hidden_down, 'narrow', axis=0, tiled=True)  14.4 us
    all_gather x1, blocking collectives, body(): lax.all_gather(hidden_up, 'narrow', axis=0, tiled=True)  14.3 us
    all_to_all x1, blocking collectives, exchange_blocks(): blocks = lax.all_to_all(blocks, name, split_axis=0, concat_axis=0)  14.2 us
    all_gather x1, blocking collectives, body(): lax.all_gather(sample_in, 'narrow', axis=0, tiled=True)  13.8 us
  transfers between devices with their start and end apart: 1, of which 0 were waited for; matrix products, arithmetic and copies ran while one was open for 0% of the time, Pallas kernels for 0%

profile of v1, /device:TPU:0, one launch (start us, length us, event | category | flops | bytes accessed | tf_op | source)
XLA Modules:
  0.0 165.8 jit_solution(11421872775888402559)
XLA Ops:
  0.0 0.8 fusion.126
  0.8 15.2 %all_gather.19 = bf16[192,192]{1,0:T(8,128)(2,1)S(1)} all-gather(bf16[48,192]{1,0:T(8,128)(2,1)} %param.19), channel_id=1, replica_groups=mesh['groups'=1,'wide'=8,'narrow'=4] {'narrow'}, dimensions={0}, use_global_device_ids=true | all-gather | bytes 92160 | tf_op jit(solution)/shard_map/all_gather | solution.py:69
  16.0 14.4 %all_gather.18 = bf16[192,576]{1,0:T(8,128)(2,1)S(1)} all-gather(bf16[48,576]{1,0:T(8,128)(2,1)} %param.18), channel_id=1, replica_groups=mesh['groups'=1,'wide'=8,'narrow'=4] {'narrow'}, dimensions={0}, use_global_device_ids=true | all-gather | bytes 276480 | tf_op jit(solution)/shard_map/all_gather | solution.py:68
  30.5 1.3 convolution_convert_fusion.3
  31.8 9.3 %while.22 = (s32[]{:T(128)}, bf16[4,128,192]{1,2,0:T(8,128)(2,1)S(1)}, bf16[4,128,576]{1,2,0:T(8,128)(2,1)S(1)}, s32[4]{0:T(128)S(1)}, s32[]{:T(128)}) while((s32[]{:T(128)}, bf16[4,128,192]{1,2,0:T(8,128)(2,1)S(1)}, bf16[4,128,576]{1,2,0:T(8,128)(2,1)S(1)}, s32[4]{0:T(128)S(1)}, s32[]{:T(128)}) %tuple.61), condition=%wide.region_3.4_spmd.clone, body=%wide.region_0.3_spmd.clone.sunk | while | flops 19981440 | bytes 1776221 | solution.py:77
  41.6 0.9 copy.108
  42.5 5.3 %all-to-all-start = ((bf16[4,128,192]{2,0,1:T(4,128)(2,1)}), bf16[4,128,192]{2,0,1:T(4,128)(2,1)S(1)}, u32[]{:S(2)}, u32[]{:S(2)}) async-start(bf16[4,128,192]{2,0,1:T(4,128)(2,1)} %copy.108), calls=%async_computation | async-start | bytes 524288 | tf_op jit(solution)/shard_map/all_to_all | solution.py:80
  47.8 16.4 %all_gather.21 = bf16[192,192]{1,0:T(8,128)(2,1)S(1)} all-gather(bf16[48,192]{1,0:T(8,128)(2,1)S(1)} %copy-done.4), channel_id=1, replica_groups=mesh['groups'=1,'wide'=8,'narrow'=4] {'narrow'}, dimensions={0}, use_global_device_ids=true | all-gather | bytes 92160 | tf_op jit(solution)/shard_map/all_gather | solution.py:84
  64.3 13.8 %all_gather.20 = bf16[192,576]{1,0:T(8,128)(2,1)S(1)} all-gather(bf16[48,576]{1,0:T(8,128)(2,1)S(1)} %copy-done.3), channel_id=1, replica_groups=mesh['groups'=1,'wide'=8,'narrow'=4] {'narrow'}, dimensions={0}, use_global_device_ids=true | all-gather | bytes 276480 | tf_op jit(solution)/shard_map/all_gather | solution.py:83
  78.0 14.3 %all_gather.22 = bf16[192,768]{1,0:T(8,128)(2,1)S(1)} all-gather(bf16[48,768]{1,0:T(8,128)(2,1)S(1)} %copy-done.2), channel_id=1, replica_groups=mesh['groups'=1,'wide'=8,'narrow'=4] {'narrow'}, dimensions={0}, use_global_device_ids=true | all-gather | bytes 368640 | tf_op jit(solution)/shard_map/all_gather | solution.py:95
  92.3 14.4 %all_gather.23 = bf16[768,192]{1,0:T(8,128)(2,1)S(1)} all-gather(bf16[192,192]{1,0:T(8,128)(2,1)S(1)} %copy-done.1), channel_id=1, replica_groups=mesh['groups'=1,'wide'=8,'narrow'=4] {'narrow'}, dimensions={0}, use_global_device_ids=true | all-gather | bytes 368640 | tf_op jit(solution)/shard_map/all_gather | solution.py:96
  107.4 6.4 %while.23 = (s32[]{:T(128)}, bf16[4,128,192]{1,2,0:T(8,128)(2,1)S(1)}, bf16[4,128,576]{1,2,0:T(8,128)(2,1)S(1)}, s32[]{:T(128)}, s32[]{:T(128)}) while((s32[]{:T(128)}, bf16[4,128,192]{1,2,0:T(8,128)(2,1)S(1)}, bf16[4,128,576]{1,2,0:T(8,128)(2,1)S(1)}, s32[]{:T(128)}, s32[]{:T(128)}) %tuple.58), condition=%wide.region_9.10_spmd.clone, body=%wide.region_6.9_spmd.clone.sunk | while | flops 19981440 | bytes 1776209 | solution.py:89
  114.4 0.8 fusion.43
  115.2 3.8 %fusion.46 = (f32[4,128]{1,0:T(4,128)S(1)}, f32[4,128,192]{1,2,0:T(8,128)S(1)}) fusion(bf16[4,128,192]{1,2,0:T(8,128)(2,1)S(1)} %multiply_convert_fusion, bf16[768,192]{1,0:T(8,128)(2,1)S(1)} %all_gather.23, f32[4,128,768]{2,1,0:T(8,128)S(1)} %get-tuple-element.114, u8[128,768]{1,0:T(8,128)(4,1)S(1)} %get-tuple-element.78, ...), kind=kOutput, calls=%fused_computation.80 | convolution fusion | flops 178814464 | bytes 2656256 | tf_op jit(solution)/shard_map/dot_general | solution.py:49
  119.9 0.8 fusion.81
  120.7 0.8 fusion.80
  121.5 0.8 fusion.79
  122.3 0.8 fusion.78
  123.1 0.8 fusion.77
  123.9 0.8 fusion.76
  124.7 0.8 fusion.75
  125.5 0.8 fusion.74
  126.3 0.8 fusion.73
  127.1 0.8 fusion.72
  127.9 0.8 fusion.71
  128.7 0.8 fusion.70
  129.4 0.8 fusion.69
  130.2 0.8 fusion.68
  131.0 0.8 fusion.67
  131.9 0.8 fusion.66
  132.7 0.8 fusion.65
  133.5 0.8 fusion.64
  134.2 0.8 fusion.63
  135.0 0.8 fusion.62
  135.8 0.8 fusion.61
  136.6 0.8 fusion.60
  137.4 0.8 fusion.59
  138.2 0.8 fusion.58
  139.0 0.8 fusion.57
  139.8 0.8 fusion.56
  140.6 0.8 fusion.55
  141.4 0.8 fusion.54
  142.2 0.8 fusion.53
  143.0 0.8 fusion.52
  143.9 0.8 fusion.51
  144.7 5.9 %copy.113 = bf16[32,4,4,192]{3,2,1,0:T(4,128)(2,1)S(1)} copy(bf16[32,4,4,192]{1,3,2,0:T(8,128)(2,1)} %fusion.51) | data formatting | bytes 393216 | tf_op jit(solution)/shard_map/stack | solution.py:12
  150.6 14.2 %all_to_all.23 = bf16[32,4,4,192]{3,2,1,0:T(4,128)(2,1)S(1)} all-to-all(bf16[32,4,4,192]{3,2,1,0:T(4,128)(2,1)S(1)} %copy.113), channel_id=1, replica_groups=mesh['groups'=1,'wide'=8,'narrow'=4] {'wide','narrow'}, dimensions={0} | all-to-all | bytes 393216 | tf_op jit(solution)/shard_map/all_to_all | solution.py:13
  164.9 0.9 copy.115
  (94 shorter events, 18.0 us)
Async XLA Ops:
  0.0 31.8 %copy-start.5 = (s32[4]{0:T(128)S(1)}, s32[4]{0:T(128)}, u32[]{:S(2)}) copy-start(s32[4]{0:T(128)} %param.15) | copy-start | bytes 52
  31.8 9.3 %copy-start = (bf16[4,128,192]{1,2,0:T(8,128)(2,1)S(1)}, bf16[4,128,192]{1,2,0:T(8,128)(2,1)}, u32[]{:S(2)}) copy-start(bf16[4,128,192]{1,2,0:T(8,128)(2,1)} %param.14) | copy-start | bytes 589828
  41.1 6.7 %copy-start.4 = (bf16[48,192]{1,0:T(8,128)(2,1)S(1)}, bf16[48,192]{1,0:T(8,128)(2,1)}, u32[]{:S(2)}) copy-start(bf16[48,192]{1,0:T(8,128)(2,1)} %param.21) | copy-start | bytes 55300
  41.1 23.2 %copy-start.3 = (bf16[48,576]{1,0:T(8,128)(2,1)S(1)}, bf16[48,576]{1,0:T(8,128)(2,1)}, u32[]{:S(2)}) copy-start(bf16[48,576]{1,0:T(8,128)(2,1)} %param.20) | copy-start | bytes 165892
  41.1 36.9 %copy-start.2 = (bf16[48,768]{1,0:T(8,128)(2,1)S(1)}, bf16[48,768]{1,0:T(8,128)(2,1)}, u32[]{:S(2)}) copy-start(bf16[48,768]{1,0:T(8,128)(2,1)} %param.22) | copy-start | bytes 221188
  41.4 50.9 %copy-start.1 = (bf16[192,192]{1,0:T(8,128)(2,1)S(1)}, bf16[192,192]{1,0:T(8,128)(2,1)}, u32[]{:S(2)}) copy-start(bf16[192,192]{1,0:T(8,128)(2,1)} %param.23) | copy-start | bytes 221188
  42.5 64.2 %all-to-all-start = ((bf16[4,128,192]{2,0,1:T(4,128)(2,1)}), bf16[4,128,192]{2,0,1:T(4,128)(2,1)S(1)}, u32[]{:S(2)}, u32[]{:S(2)}) async-start(bf16[4,128,192]{2,0,1:T(4,128)(2,1)} %copy.108), calls=%async_computation | async-start | bytes 524288 | tf_op jit(solution)/shard_map/all_to_all | solution.py:80
